TPU v7x, 128 devices: a whole 4x4x4 slice. The times are simulated.
128 devices in a mesh: pool: 32 (over x, z, core), exp: 4 (over y).
Axes of the slice: x: 4, y: 4, z: 4, core: 2. Of those that a mesh axis runs over, the one named last changes fastest.
Arguments:
- tokens: bfloat16 [512, 1024], P('pool'), as said below
- block_table: int32 [512, 128], replicated, may hold values from -1 to 4607, as said below
- lengths: int32 [512], replicated, may hold values from 1 to 16384, as said below
- k_cache: bfloat16 [4096, 128, 512], P('pool', None, 'exp'), as said below
- v_cache: bfloat16 [4096, 128, 512], P('pool', None, 'exp'), may hold values from -9 to 9
- hidden_store: bfloat16 [512, 128, 1024], P('pool'), may hold values from -6 to 6
- norm_attn: bfloat16 [1024], replicated, may hold values from 0.5 to 1.5
- w_query: bfloat16 [1024, 1024], P(None, 'exp'), as said below
- w_key: bfloat16 [1024, 512], P(None, 'exp'), may hold values from -0.1875 to 0.1875
- w_value: bfloat16 [1024, 512], P(None, 'exp'), may hold values from -0.1875 to 0.1875
- w_out: bfloat16 [1024, 1024], P('exp'), may hold values from -0.1875 to 0.1875
- norm_moe: bfloat16 [1024], replicated, may hold values from 0.5 to 1.5
- expert_ids: int32 [512, 8], P('pool'), may hold values from 0 to 31, all different within a row; in each aligned block of 16 rows (0 to 15, 16 to 31, ...) at most 8 rows name the same one
- gate_weights: float32 [512, 8], P('pool'), may hold values from 0.1 to 1
- w_gate: bfloat16 [32, 1024, 512], P('pool'), may hold values from -0.1875 to 0.1875
- w_up: bfloat16 [32, 1024, 512], P('pool'), may hold values from -0.1875 to 0.1875
- w_down: bfloat16 [32, 512, 1024], P('pool'), may hold values from -0.25 to 0.25
Outputs:
- layer_out: bfloat16 [512, 1024], P('pool', 'exp')
Inputs may be any that keep to these rules, and one draw needn't show every extreme that they name: `block_table`: every block number 0 to 4607 stands exactly once in the table; a request's blocks fill the start of its row and -1 fills the rest; each request has 1 to 128 blocks and some request has exactly 128. `lengths`: A request with n blocks has a length above (n - 1) * 128 and at most n * 128; some request has the length 16384. `expert_ids`: in the rows of one pool index no expert is named by more than 8 rows. `tokens`: entries lie within -8 to 8. `k_cache`: entries lie within -8 to 8. `w_query`: entries are of magnitude below 7 / sqrt(1024).
All inputs are finite; a program needn't handle non-finite values.
Results may differ from a plain program's by a relative error of at most 0.009.
Values may be sent and summed in bfloat16 or wider, within the bound.
No kernel may reach another device: no remote copies, remote signals or barrier semaphores. Data moves between devices by JAX's collectives and lax.ppermute only.
A program may use at most 128 MiB of HBM per device.

v0:
```python
import jax
import jax.numpy as jnp
from jax import lax
from jax.sharding import PartitionSpec as P

HEAD_SIZE = 64
NEG_FILL = -1e30
EPSILON = 1e-05
SCORE_SCALE = 0.125
HIGHEST = lax.Precision.HIGHEST


def merged(value, axis, join):
    pieces = jax.tree.map(lambda part: lax.all_gather(part, axis), value)
    head = jax.tree.map(lambda part: part[0], pieces)
    tail = jax.tree.map(lambda part: part[1:], pieces)
    so_far, _ = lax.scan(lambda so_far, piece: (join(so_far, piece), None), head, tail)
    return so_far


def rms_scale(row_vals, gain_row):
    mean_sq = jnp.mean(row_vals * row_vals, axis=-1, keepdims=True)
    return row_vals * lax.rsqrt(mean_sq + EPSILON) * gain_row


def merge_pair(first, second):
    top_a, sum_a, out_a = first
    top_b, sum_b, out_b = second
    row_top = jnp.maximum(top_a, top_b)
    weight_a = jnp.exp(top_a - row_top)
    weight_b = jnp.exp(top_b - row_top)
    spread = out_a.shape[-1] // top_a.shape[-1]
    merged_out = out_a * jnp.repeat(weight_a, spread, axis=-1) + out_b * jnp.repeat(
        weight_b, spread, axis=-1
    )
    return (row_top, sum_a * weight_a + sum_b * weight_b, merged_out)


def on_device(
    tokens,
    block_table,
    lengths,
    k_cache,
    v_cache,
    hidden_store,
    norm_attn,
    w_query,
    w_key,
    w_value,
    w_out,
    norm_moe,
    expert_ids,
    gate_weights,
    w_gate,
    w_up,
    w_down,
):
    pool_count = lax.axis_size("pool")
    exp_count = lax.axis_size("exp")
    pool_index = lax.axis_index("pool")
    exp_index = lax.axis_index("exp")
    req_dev = tokens.shape[0]
    model_width = tokens.shape[1]
    quarter = model_width // exp_count
    x_rows = tokens.astype(jnp.float32)
    normed = rms_scale(x_rows, norm_attn.astype(jnp.float32)).astype(jnp.bfloat16)
    queries = jnp.dot(normed, w_query, preferred_element_type=jnp.float32).astype(jnp.bfloat16)
    all_queries = lax.all_gather(queries, "pool", axis=0, tiled=True)
    stored_rows = hidden_store.reshape(-1, model_width)
    stored_shape = (hidden_store.shape[0], hidden_store.shape[1], w_key.shape[1])
    key_new = (
        jnp.dot(stored_rows, w_key, preferred_element_type=jnp.float32)
        .astype(jnp.bfloat16)
        .reshape(stored_shape)
    )
    value_new = (
        jnp.dot(stored_rows, w_value, preferred_element_type=jnp.float32)
        .astype(jnp.bfloat16)
        .reshape(stored_shape)
    )
    keys_here = jnp.concatenate([k_cache, key_new], axis=0)
    values_here = jnp.concatenate([v_cache, value_new], axis=0)
    slot_count, page_len, key_width = keys_here.shape
    query_width = queries.shape[1]
    kv_groups = key_width // HEAD_SIZE
    per_group = query_width // key_width
    head_count = query_width // HEAD_SIZE
    requests = block_table.shape[0]
    list_len = block_table.shape[1]
    flat_ids = block_table.reshape(-1)
    entry_index = jnp.arange(requests * list_len, dtype=jnp.int32)
    global_slot = pool_index * slot_count + jnp.arange(slot_count, dtype=jnp.int32)
    found_entry = jnp.sum(
        jnp.where(flat_ids[None, :] == global_slot[:, None], entry_index[None, :], 0), axis=1
    )
    slot_req = found_entry // list_len
    slot_block = found_entry % list_len
    member = slot_req[:, None] == jnp.arange(requests, dtype=jnp.int32)[None, :]
    member_low = member.astype(jnp.bfloat16)
    slot_queries = jnp.dot(member_low, all_queries, preferred_element_type=jnp.float32).astype(
        jnp.bfloat16
    )
    slot_length = jnp.sum(jnp.where(member, lengths[None, :], 0), axis=1)
    q_grouped = slot_queries.reshape(slot_count, kv_groups, per_group, HEAD_SIZE)
    k_grouped = keys_here.reshape(slot_count, page_len, kv_groups, HEAD_SIZE)
    v_grouped = values_here.reshape(slot_count, page_len, kv_groups, HEAD_SIZE)
    scores = (
        jnp.einsum("sgqd,stgd->sgqt", q_grouped, k_grouped, preferred_element_type=jnp.float32)
        * SCORE_SCALE
    )
    positions = slot_block[:, None] * page_len + jnp.arange(page_len, dtype=jnp.int32)[None, :]
    is_valid = (positions < slot_length[:, None])[:, None, None, :]
    masked = jnp.where(is_valid, scores, NEG_FILL)
    block_top = jnp.max(masked, axis=-1)
    weights = jnp.where(is_valid, jnp.exp(masked - block_top[..., None]), 0.0)
    block_sum = jnp.sum(weights, axis=-1)
    block_out = jnp.einsum(
        "sgqt,stgd->sgqd",
        weights.astype(jnp.bfloat16),
        v_grouped,
        preferred_element_type=jnp.float32,
    )
    slot_top = block_top.reshape(slot_count, head_count)
    slot_sum = block_sum.reshape(slot_count, head_count)
    slot_out = block_out.reshape(slot_count, query_width)
    local_top = jnp.max(jnp.where(member[:, :, None], slot_top[:, None, :], NEG_FILL), axis=0)
    own_top = jnp.max(jnp.where(member[:, :, None], local_top[None, :, :], NEG_FILL), axis=1)
    factor = jnp.exp(slot_top - own_top)
    one_hot = member.astype(jnp.float32)
    local_sum = jnp.einsum("sr,sh->rh", one_hot, slot_sum * factor, precision=HIGHEST)
    local_out = jnp.einsum(
        "sr,sc->rc", one_hot, slot_out * jnp.repeat(factor, HEAD_SIZE, axis=1), precision=HIGHEST
    )
    all_top, all_sum, all_out = merged((local_top, local_sum, local_out), "pool", merge_pair)
    row_start = pool_index * req_dev
    total_sum = lax.dynamic_slice_in_dim(all_sum, row_start, req_dev, 0)
    accum = lax.dynamic_slice_in_dim(all_out, row_start, req_dev, 0)
    attended = (accum / jnp.repeat(total_sum, HEAD_SIZE, axis=-1)).astype(jnp.bfloat16)
    projected = lax.psum(jnp.dot(attended, w_out, preferred_element_type=jnp.float32), "exp")
    mixed = x_rows + projected
    normed_moe = rms_scale(mixed, norm_moe.astype(jnp.float32)).astype(jnp.bfloat16)
    top_count = expert_ids.shape[1]
    capacity = min(req_dev, 2 * ((req_dev * top_count + pool_count - 1) // pool_count))
    route_flat = expert_ids.reshape(-1)
    expert_hit = (route_flat[:, None] == jnp.arange(pool_count, dtype=jnp.int32)[None, :]).astype(
        jnp.int32
    )
    slot_rank = jnp.sum(jnp.cumsum(expert_hit, axis=0) * expert_hit, axis=1) - 1
    slot_pos = route_flat * capacity + slot_rank
    placed = (
        slot_pos[:, None] == jnp.arange(pool_count * capacity, dtype=jnp.int32)[None, :]
    ).astype(jnp.float32)
    placed = placed.reshape(req_dev, top_count, pool_count * capacity)
    send_map = jnp.sum(placed, axis=1).astype(jnp.bfloat16)
    combine_map = jnp.einsum("tk,tkc->tc", gate_weights, placed, precision=HIGHEST)
    outgoing = jnp.einsum("tc,td->cd", send_map, normed_moe, preferred_element_type=jnp.float32)
    outgoing = outgoing.astype(jnp.bfloat16).reshape(pool_count, capacity, model_width)
    arrived = lax.all_to_all(outgoing, "pool", split_axis=0, concat_axis=0, tiled=True)
    sources = arrived.shape[0]
    slots_here = arrived.shape[1]
    row_block = arrived.reshape(-1, model_width)
    gate_act = jnp.dot(row_block, w_gate[0], preferred_element_type=jnp.float32)
    up_act = jnp.dot(row_block, w_up[0], preferred_element_type=jnp.float32)
    hidden = (jax.nn.silu(gate_act) * up_act).astype(jnp.bfloat16)
    expert_low = jnp.dot(hidden, w_down[0], preferred_element_type=jnp.float32).astype(jnp.bfloat16)
    expert_low = expert_low.reshape(sources, slots_here, model_width)
    expert_out = lax.dynamic_slice_in_dim(expert_low, exp_index * quarter, quarter, 2)
    returned = lax.all_to_all(expert_out, "pool", split_axis=0, concat_axis=0, tiled=True)
    moe_share = jnp.dot(
        combine_map,
        returned.reshape(pool_count * capacity, quarter).astype(jnp.float32),
        precision=HIGHEST,
    )
    mixed_share = lax.dynamic_slice_in_dim(mixed, exp_index * quarter, quarter, 1)
    return (mixed_share + moe_share).astype(jnp.bfloat16)


def solution(mesh):
    placed = (
        P("pool", None),
        P(),
        P(),
        P("pool", None, "exp"),
        P("pool", None, "exp"),
        P("pool", None, None),
        P(),
        P(None, "exp"),
        P(None, "exp"),
        P(None, "exp"),
        P("exp", None),
        P(),
        P("pool", None),
        P("pool", None),
        P("pool", None, None),
        P("pool", None, None),
        P("pool", None, None),
    )
    return jax.shard_map(
        on_device, mesh=mesh, in_specs=placed, out_specs=P("pool", "exp"), check_vma=False
    )
```

profile of v0, /device:TPU:1, one launch (start us, length us, event | category | flops | bytes accessed | tf_op | source)
XLA Modules:
  0.0 319.9 jit_solution(11277620771074689597)
XLA Ops:
  6.5 6.6 %select_reduce_fusion = s32[144]{0:T(256)S(1)} fusion(s32[65536]{0:T(1024)} %bitcast.87, s32[144]{0:T(256)S(1)} %iota_add_fusion), kind=kLoop, calls=%fused_computation.10 | loop fusion | flops 28311408 | bytes 263296 | tf_op jit(solution)/shard_map/reduce_sum | solution.py:93
  13.3 0.9 select_reduce_fusion.3
  14.9 0.9 fusion.46
  15.8 1.3 convolution_convert_fusion.5
  17.1 27.6 %all_gather.21 = bf16[512,256]{1,0:T(8,128)(2,1)S(1)} all-gather(bf16[16,256]{1,0:T(8,128)(2,1)S(1)} %convolution_convert_fusion.5), channel_id=1, replica_groups=mesh['pool'=32,'exp'=4] {'pool'}, dimensions={0}, use_global_device_ids=true | all-gather | bytes 270336 | tf_op jit(solution)/shard_map/all_gather | solution.py:68
  45.1 3.5 %convolution_convert_fusion.1 = bf16[2048,128]{1,0:T(8,128)(2,1)S(1)} fusion(bf16[2048,1024]{1,0:T(8,128)(2,1)} %bitcast.89, bf16[1024,128]{1,0:T(8,128)(2,1)} %param.27), kind=kOutput, calls=%fused_computation.20 | convolution fusion | flops 537133056 | bytes 4980736 | tf_op jit(solution)/shard_map/dot_general | solution.py:72
  49.6 6.4 %copy.75 = bf16[128,128,128]{1,2,0:T(8,128)(2,1)} copy(bf16[128,128,128]{2,1,0:T(8,128)(2,1)} %param.22) | data formatting | bytes 8388608 | tf_op args[3]
  56.1 3.7 %fusion.67 = (f32[144,2,2]{2,1,0:T(2,128)S(1)}, f32[144,2,2,128]{3,2,1,0:T(2,128)S(1)}) fusion(bf16[144,2,2,64]{3,2,1,0:T(2,128)(2,1)S(1)} %reshape.185, bf16[16,128,2,64]{1,3,2,0:T(8,128)(2,1)S(1)} %copy.77, bf16[128,128,2,64]{1,3,2,0:T(8,128)(2,1)} %bitcast.84, pred[144,128]{1,0:T(8,128)(4,1)S(1)} %add_compare_fusion), kind=kOutput, calls=%fused_computation.105 | convolution fusion | flops 12017088 | bytes 5107968 | tf_op jit(solution)/shard_map/sgqd,stgd->sgqt/dot_general | solution.py:108
  61.0 3.4 %convolution_convert_fusion = bf16[2048,128]{1,0:T(8,128)(2,1)S(1)} fusion(bf16[2048,1024]{1,0:T(8,128)(2,1)} %bitcast.90, bf16[1024,128]{1,0:T(8,128)(2,1)S(1)} %copy-done.6), kind=kOutput, calls=%fused_computation.19 | convolution fusion | flops 537133056 | bytes 4980736 | tf_op jit(solution)/shard_map/dot_general | solution.py:77
  65.5 6.4 %copy.80 = bf16[128,128,128]{1,2,0:T(8,128)(2,1)} copy(bf16[128,128,128]{2,1,0:T(8,128)(2,1)} %param.23) | data formatting | bytes 8388608 | tf_op args[4]
  71.9 4.8 %fusion.7 = f32[144,2,2,64]{3,2,1,0:T(2,128)S(1)} fusion(bf16[16,128,2,64]{1,3,2,0:T(8,128)(2,1)S(1)} %copy.82, bf16[128,128,2,64]{1,3,2,0:T(8,128)(2,1)} %bitcast.85, f32[144,2,2,128]{3,2,1,0:T(2,128)S(1)} %get-tuple-element.103, pred[144,128]{1,0:T(8,128)(4,1)S(1)} %add_compare_fusion, f32[144,2,2]{2,1,0:T(2,128)S(1)} %get-tuple-element.102), kind=kOutput, calls=%fused_computation.15 | convolution fusion | flops 12017664 | bytes 5181696 | tf_op jit(solution)/shard_map/sgqt,stgd->sgqd/dot_general | solution.py:117
  77.0 1.5 fusion.35
  78.6 0.9 fusion.60
  79.9 24.3 %all-gather.1 = f32[16384,4]{0,1:T(4,128)S(1)} all-gather(f32[512,4]{0,1:T(4,128)S(1)} %fusion.36), channel_id=3, replica_groups=mesh['pool'=32,'exp'=4] {'pool'}, dimensions={0}, use_global_device_ids=true | all-gather | bytes 270336 | tf_op jit(solution)/shard_map/all_gather | solution.py:14
  104.3 22.6 %all-gather = f32[16384,4]{0,1:T(4,128)S(1)} all-gather(f32[512,4]{0,1:T(4,128)S(1)} %select_reduce_fusion.2), channel_id=2, replica_groups=mesh['pool'=32,'exp'=4] {'pool'}, dimensions={0}, use_global_device_ids=true | all-gather | bytes 270336 | tf_op jit(solution)/shard_map/all_gather | solution.py:14
  128.3 23.1 %all-gather.5.cloned.1.call-done = f32[16384,256]{1,0:T(8,128)} async-done(((f32[512,256]{1,0:T(8,128)}), f32[16384,256]{1,0:T(8,128)}) %all-gather.5.cloned.1.call-update) | async-done | bytes 16777232 | tf_op jit(solution)/shard_map/all_gather | solution.py:14
  151.4 1.1 slice.32
  152.7 11.1 %slice.35 = f32[15872,256]{1,0:T(8,128)} slice(f32[16384,256]{1,0:T(8,128)} %all-gather.5.cloned.1.call-done), slice={[512:16384], [0:256]} | slice | bytes 32505856 | tf_op jit(solution)/shard_map/slice | solution.py:16
  163.9 70.2 %while.14 = (s32[]{:T(128)}, f32[512,4]{0,1:T(4,128)S(1)}, f32[512,4]{0,1:T(4,128)S(1)}, f32[512,256]{0,1:T(8,128)S(1)}, f32[31,512,4]{1,2,0:T(4,128)}, /*index=...) while((s32[]{:T(128)}, f32[512,4]{0,1:T(4,128)S(1)}, f32[512,4]{0,1:T(4,128)S(1)}, ...), condition=%wide.region_8.9_spmd, body=%wide.region_7.8_spmd.sunk | while | flops 405506 | bytes 3752029 | solution.py:17
  163.9 0.8 fusion.82
  164.7 1.1 constant_dynamic-slice_fusion.4
  166.9 1.1 constant_dynamic-slice_fusion.4
  168.5 0.7 fusion.82
  169.2 1.1 constant_dynamic-slice_fusion.4
  170.7 0.7 fusion.82
  171.5 1.1 constant_dynamic-slice_fusion.4
  173.7 1.1 constant_dynamic-slice_fusion.4
  176.0 1.1 constant_dynamic-slice_fusion.4
  178.2 1.1 constant_dynamic-slice_fusion.4
  180.5 1.1 constant_dynamic-slice_fusion.4
  182.8 1.1 constant_dynamic-slice_fusion.4
  185.0 1.1 constant_dynamic-slice_fusion.4
  187.3 1.1 constant_dynamic-slice_fusion.4
  189.6 1.1 constant_dynamic-slice_fusion.4
  191.8 1.1 constant_dynamic-slice_fusion.4
  194.1 1.1 constant_dynamic-slice_fusion.4
  196.4 1.1 constant_dynamic-slice_fusion.4
  198.6 1.1 constant_dynamic-slice_fusion.4
  200.9 1.1 constant_dynamic-slice_fusion.4
  203.1 1.1 constant_dynamic-slice_fusion.4
  205.4 1.1 constant_dynamic-slice_fusion.4
  207.7 1.1 constant_dynamic-slice_fusion.4
  209.9 1.1 constant_dynamic-slice_fusion.4
  212.2 1.1 constant_dynamic-slice_fusion.4
  214.5 1.1 constant_dynamic-slice_fusion.4
  216.7 1.1 constant_dynamic-slice_fusion.4
  219.0 1.1 constant_dynamic-slice_fusion.4
  221.3 1.1 constant_dynamic-slice_fusion.4
  223.5 1.1 constant_dynamic-slice_fusion.4
  225.8 1.1 constant_dynamic-slice_fusion.4
  228.0 1.1 constant_dynamic-slice_fusion.4
  230.3 1.1 constant_dynamic-slice_fusion.4
  232.6 1.1 constant_dynamic-slice_fusion.4
  234.3 0.8 fusion.68
  235.3 37.8 %all-reduce.2.cloned.1.call-done = f32[16,1024]{1,0:T(8,128)} async-done(((f32[16,1024]{1,0:T(8,128)}), f32[16,1024]{1,0:T(8,128)}) %all-reduce.2.cloned.1.call-update) | async-done | bytes 65552 | tf_op jit(solution)/shard_map/psum | solution.py:139
  273.1 1.0 multiply_reduce_fusion
  274.1 1.1 fusion.11
  275.2 9.7 %all-to-all-start = ((bf16[32,8,1024]{2,1,0:T(8,128)(2,1)}), bf16[32,8,1024]{2,1,0:T(8,128)(2,1)S(1)}, u32[]{:S(2)}, u32[]{:S(2)}) async-start(bf16[32,8,1024]{2,1,0:T(8,128)(2,1)} %fusion.11), calls=%async_computation | async-start | bytes 1048576 | tf_op jit(solution)/shard_map/all_to_all | solution.py:158
  285.0 11.5 %all-to-all-done = bf16[32,8,1024]{2,1,0:T(8,128)(2,1)S(1)} async-done(((bf16[32,8,1024]{2,1,0:T(8,128)(2,1)}), bf16[32,8,1024]{2,1,0:T(8,128)(2,1)S(1)}, u32[]{:S(2)}, u32[]{:S(2)}) %all-to-all-start) | async-done | bytes 524320 | tf_op jit(solution)/shard_map/all_to_all | solution.py:158
  296.5 1.7 fusion.20
  298.2 2.0 fusion.12
  300.9 3.6 %all-to-all-start.1 = ((bf16[32,8,256]{2,1,0:T(8,128)(2,1)}), bf16[32,8,256]{2,1,0:T(8,128)(2,1)S(1)}, u32[]{:S(2)}, u32[]{:S(2)}) async-start(bf16[32,8,256]{2,1,0:T(8,128)(2,1)} %constant_dynamic-slice_fusion.2), calls=%async_computation.1 | async-start | bytes 262144 | tf_op jit(solution)/shard_map/all_to_all | solution.py:168
  304.8 7.4 %all-to-all-done.1 = bf16[32,8,256]{2,1,0:T(8,128)(2,1)S(1)} async-done(((bf16[32,8,256]{2,1,0:T(8,128)(2,1)}), bf16[32,8,256]{2,1,0:T(8,128)(2,1)S(1)}, u32[]{:S(2)}, u32[]{:S(2)}) %all-to-all-start.1) | async-done | bytes 131104 | tf_op jit(solution)/shard_map/all_to_all | solution.py:168
  312.2 0.8 fusion.17
  (153 shorter events, 41.9 us)
Async XLA Ops:
  6.5 291.6 %copy-start = (bf16[1,512,1024]{2,1,0:T(8,128)(2,1)S(1)}, bf16[1,512,1024]{2,1,0:T(8,128)(2,1)}, u32[]{:S(2)}) copy-start(bf16[1,512,1024]{2,1,0:T(8,128)(2,1)} %param.35) | copy-start | bytes 3145732
  6.5 144.9 %all-gather.5.cloned.1.call-start = ((), (), s32[]{:S(2)}) async-start(), calls=%async_computation.3 | async-start | bytes 17301504 | tf_op jit(solution)/shard_map/all_gather | solution.py:14
  56.1 4.9 %copy-start.6 = (bf16[1024,128]{1,0:T(8,128)(2,1)S(1)}, bf16[1024,128]{1,0:T(8,128)(2,1)}, u32[]{:S(2)}) copy-start(bf16[1024,128]{1,0:T(8,128)(2,1)} %param.28) | copy-start | bytes 786436
  76.7 50.9 %copy-start.3 = (s32[16,8]{0,1:T(8,128)S(1)}, s32[16,8]{0,1:T(8,128)}, u32[]{:S(2)}) copy-start(s32[16,8]{0,1:T(8,128)} %param.31) | copy-start | bytes 1540
  76.7 51.6 %copy-start.5 = (bf16[1024]{0:T(1024)(128)(2,1)S(1)}, bf16[1024]{0:T(1024)(128)(2,1)}, u32[]{:S(2)}) copy-start(bf16[1024]{0:T(1024)(128)(2,1)} %param.30) | copy-start | bytes 6148
  78.5 194.6 %all-reduce.2.cloned.1.call-start = ((), (), s32[]{:S(2)}) async-start(), calls=%async_computation.2 | async-start | bytes 131072 | tf_op jit(solution)/shard_map/psum | solution.py:139
  163.9 70.4 %copy-start.1 = (bf16[256,1024]{1,0:T(8,128)(2,1)S(1)}, bf16[256,1024]{1,0:T(8,128)(2,1)}, u32[]{:S(2)}) copy-start(bf16[256,1024]{1,0:T(8,128)(2,1)} %param.29) | copy-start | bytes 1572868
  163.9 109.2 %copy-start.2 = (bf16[16,1024]{1,0:T(8,128)(2,1)S(1)}, bf16[16,1024]{1,0:T(8,128)(2,1)}, u32[]{:S(2)}) copy-start(bf16[16,1024]{1,0:T(8,128)(2,1)} %param.19) | copy-start | bytes 98308
  163.9 121.0 %copy-start.4 = (f32[16,8]{0,1:T(8,128)S(1)}, f32[16,8]{0,1:T(8,128)}, u32[]{:S(2)}) copy-start(f32[16,8]{0,1:T(8,128)} %param.32) | copy-start | bytes 1540
  275.2 21.3 %all-to-all-start = ((bf16[32,8,1024]{2,1,0:T(8,128)(2,1)}), bf16[32,8,1024]{2,1,0:T(8,128)(2,1)S(1)}, u32[]{:S(2)}, u32[]{:S(2)}) async-start(bf16[32,8,1024]{2,1,0:T(8,128)(2,1)} %fusion.11), calls=%async_computation | async-start | bytes 1048576 | tf_op jit(solution)/shard_map/all_to_all | solution.py:158
  300.9 11.3 %all-to-all-start.1 = ((bf16[32,8,256]{2,1,0:T(8,128)(2,1)}), bf16[32,8,256]{2,1,0:T(8,128)(2,1)S(1)}, u32[]{:S(2)}, u32[]{:S(2)}) async-start(bf16[32,8,256]{2,1,0:T(8,128)(2,1)} %constant_dynamic-slice_fusion.2), calls=%async_computation.1 | async-start | bytes 262144 | tf_op jit(solution)/shard_map/all_to_all | solution.py:168
Sparse Core Ops, SparseCore 0:
  78.6 72.7 all-gather.4
  235.3 37.7 all-reduce.1
where the time goes:
time: 324 us; the launch traced here: 320 us
  waiting for transfers between devices  79.9 us (25%)
  blocking collectives  74.6 us (23%)
  local copies, waits for them, and re-layouts  70 us (22%)
  other arithmetic  42 us (13%)
  matrix products  25.4 us (8%)
  between operations  13.7 us (4%)
  starting transfers between devices  13.4 us (4%)
    all_gather x2, blocking collectives, merged(): pieces = jax.tree.map(lambda part: lax.all_gather(part, axis), value)  47 us
    dynamic_slice x62, local copies, waits for them, and re-layouts, merged(): lax.scan(lambda so_far, piece: (join(so_far, piece), None), head, tail)  39.6 us
    psum x1, waiting for transfers between devices, on_device(): lax.psum(jnp.dot(attended, w_out, preferred_element_type=jnp.float32), 'e...  37.8 us
    all_gather x1, blocking collectives, on_device(): all_queries = lax.all_gather(queries, 'pool', axis=0, tiled=True)  27.6 us
    all_gather x1, waiting for transfers between devices, merged(): pieces = jax.tree.map(lambda part: lax.all_gather(part, axis), value)  23.1 us
    add x31, other arithmetic, merge_pair(): return (row_top, sum_a * weight_a + sum_b * weight_b, merged_out)  22.5 us
    unnamed x18, local copies, waits for them, and re-layouts  13 us
    slice x3, local copies, waits for them, and re-layouts, merged(): tail = jax.tree.map(lambda part: part[1:], pieces)  11.9 us
  transfers between devices with their start and end apart: 4, of which 4 were waited for; matrix products, arithmetic and copies ran while one was open for 1% of the time, Pallas kernels for 0%

commit v1 on v0

--- a/solution.py
+++ b/solution.py
@@ -1,3 +1,4 @@
+import functools
 import jax
 import jax.numpy as jnp
 from jax import lax
@@ -8,6 +9,17 @@
 EPSILON = 1e-05
 SCORE_SCALE = 0.125
 HIGHEST = lax.Precision.HIGHEST
+
+
+def set_slot_over_axis(arr, dev_axis, dim_i):
+    front = lax.axis_size(dev_axis)
+    opened = jnp.concatenate(
+        lax.all_to_all(jnp.stack([arr] * front, axis=0), dev_axis, 0, 0), axis=dim_i
+    )
+    return opened
+
+
+refer_grid = functools.partial(set_slot_over_axis, dev_axis="pool", dim_i=0)
 
 
 def merged(value, axis, join):
@@ -65,7 +77,7 @@
     x_rows = tokens.astype(jnp.float32)
     normed = rms_scale(x_rows, norm_attn.astype(jnp.float32)).astype(jnp.bfloat16)
     queries = jnp.dot(normed, w_query, preferred_element_type=jnp.float32).astype(jnp.bfloat16)
-    all_queries = lax.all_gather(queries, "pool", axis=0, tiled=True)
+    all_queries = refer_grid(queries)
     stored_rows = hidden_store.reshape(-1, model_width)
     stored_shape = (hidden_store.shape[0], hidden_store.shape[1], w_key.shape[1])
     key_new = (

time: 324 us -> 306 us (0.944)
  blocking collectives: 74.6 us -> 49.3 us
  starting transfers between devices: 13.4 us -> 22.8 us
    all_gather x1 -> x0, blocking collectives: 27.6 us -> none  [on_device(): all_queries = lax.all_gather(queries, 'pool', axis=0, tiled=True)]
    all_to_all x0 -> x1, starting transfers between devices: none -> 9.43 us  [set_slot_over_axis(): lax.all_to_all(jnp.stack([arr] * front, axis=0), dev_axis, 0, 0)]
    unnamed x18 -> x22, local copies, waits for them, and re-layouts: 13 us -> 13 us
  transfers between devices with their start and end apart: 4 -> 5, of which waited for: 4 -> 4; matrix products, arithmetic and copies ran while one was open for 1% -> 10% of each run, Pallas kernels for 0% -> 0%
where the time goes in v1:
time: 306 us; the launch traced here: 302 us
  waiting for transfers between devices  79.7 us (26%)
  local copies, waits for them, and re-layouts  71.1 us (23%)
  blocking collectives  49.3 us (16%)
  other arithmetic  41.5 us (14%)
  matrix products  23.2 us (8%)
  starting transfers between devices  22.8 us (7%)
  between operations  13.8 us (5%)
    all_gather x2, blocking collectives, merged(): pieces = jax.tree.map(lambda part: lax.all_gather(part, axis), value)  49.3 us
    dynamic_slice x62, local copies, waits for them, and re-layouts, merged(): lax.scan(lambda so_far, piece: (join(so_far, piece), None), head, tail)  39.6 us
    psum x1, waiting for transfers between devices, on_device(): lax.psum(jnp.dot(attended, w_out, preferred_element_type=jnp.float32), 'e...  37.8 us
    all_gather x1, waiting for transfers between devices, merged(): pieces = jax.tree.map(lambda part: lax.all_gather(part, axis), value)  22.9 us
    add x31, other arithmetic, merge_pair(): return (row_top, sum_a * weight_a + sum_b * weight_b, merged_out)  22.5 us
    unnamed x22, local copies, waits for them, and re-layouts  13 us
    slice x3, local copies, waits for them, and re-layouts, merged(): tail = jax.tree.map(lambda part: part[1:], pieces)  12.1 us
    all_to_all x1, waiting for transfers between devices, on_device(): lax.all_to_all(outgoing, 'pool', split_axis=0, concat_axis=0, tiled=True)  11.5 us
  transfers between devices with their start and end apart: 5, of which 4 were waited for; matrix products, arithmetic and copies ran while one was open for 10% of the time, Pallas kernels for 0%

profile of v1, /device:TPU:1, one launch (start us, length us, event | category | flops | bytes accessed | tf_op | source)
XLA Modules:
  0.0 302.3 jit_solution(8689195608212112939)
XLA Ops:
  6.5 0.8 convert_element_type.59
  7.3 0.9 fusion.46
  8.2 1.3 convolution_convert_fusion.5
  9.5 0.7 stack.2
  10.2 9.4 %all-to-all-start = ((bf16[32,16,256]{2,1,0:T(8,128)(2,1)}), bf16[32,16,256]{2,1,0:T(8,128)(2,1)S(1)}, u32[]{:S(2)}, u32[]{:S(2)}) async-start(bf16[32,16,256]{2,1,0:T(8,128)(2,1)} %stack.2), calls=%async_computation | async-start | bytes 524288 | tf_op jit(solution)/shard_map/all_to_all | solution.py:17
  19.8 6.7 %select_reduce_fusion = s32[144]{0:T(256)S(1)} fusion(s32[65536]{0:T(1024)} %bitcast.89, s32[144]{0:T(256)S(1)} %iota_add_fusion), kind=kLoop, calls=%fused_computation.10 | loop fusion | flops 28311408 | bytes 263296 | tf_op jit(solution)/shard_map/reduce_sum | solution.py:105
  26.5 3.5 %convolution_convert_fusion.1 = bf16[2048,128]{1,0:T(8,128)(2,1)S(1)} fusion(bf16[2048,1024]{1,0:T(8,128)(2,1)} %bitcast.91, bf16[1024,128]{1,0:T(8,128)(2,1)} %param.27), kind=kOutput, calls=%fused_computation.20 | convolution fusion | flops 537133056 | bytes 4980736 | tf_op jit(solution)/shard_map/dot_general | solution.py:84
  30.0 1.3 convolution_convert_fusion
  32.0 0.9 copy.77
  32.8 6.4 %copy.75 = bf16[128,128,128]{1,2,0:T(8,128)(2,1)} copy(bf16[128,128,128]{2,1,0:T(8,128)(2,1)} %param.22) | data formatting | bytes 8388608 | tf_op args[3]
  40.3 6.4 %copy.80 = bf16[128,128,128]{1,2,0:T(8,128)(2,1)} copy(bf16[128,128,128]{2,1,0:T(8,128)(2,1)} %param.23) | data formatting | bytes 8388608 | tf_op args[4]
  47.2 3.7 %fusion.67 = (f32[144,2,2]{2,1,0:T(2,128)S(1)}, f32[144,2,2,128]{3,2,1,0:T(2,128)S(1)}) fusion(bf16[144,2,2,64]{3,2,1,0:T(2,128)(2,1)S(1)} %reshape.191, bf16[16,128,2,64]{1,3,2,0:T(8,128)(2,1)S(1)} %copy.77, bf16[128,128,2,64]{1,3,2,0:T(8,128)(2,1)} %bitcast.86, pred[144,128]{1,0:T(8,128)(4,1)S(1)} %add_compare_fusion), kind=kOutput, calls=%fused_computation.105 | convolution fusion | flops 12017088 | bytes 5107968 | tf_op jit(solution)/shard_map/sgqd,stgd->sgqt/dot_general | solution.py:120
  52.1 4.8 %fusion.7 = f32[144,2,2,64]{3,2,1,0:T(2,128)S(1)} fusion(bf16[16,128,2,64]{1,3,2,0:T(8,128)(2,1)S(1)} %copy.82, bf16[128,128,2,64]{1,3,2,0:T(8,128)(2,1)} %bitcast.85, f32[144,2,2,128]{3,2,1,0:T(2,128)S(1)} %get-tuple-element.103, pred[144,128]{1,0:T(8,128)(4,1)S(1)} %add_compare_fusion, f32[144,2,2]{2,1,0:T(2,128)S(1)} %get-tuple-element.102), kind=kOutput, calls=%fused_computation.15 | convolution fusion | flops 12017664 | bytes 5181696 | tf_op jit(solution)/shard_map/sgqt,stgd->sgqd/dot_general | solution.py:129
  57.2 1.5 fusion.35
  59.5 0.9 fusion.60
  60.8 25.1 %all-gather.1 = f32[16384,4]{0,1:T(4,128)S(1)} all-gather(f32[512,4]{0,1:T(4,128)S(1)} %fusion.36), channel_id=3, replica_groups=mesh['pool'=32,'exp'=4] {'pool'}, dimensions={0}, use_global_device_ids=true | all-gather | bytes 270336 | tf_op jit(solution)/shard_map/all_gather | solution.py:26
  85.9 24.2 %all-gather = f32[16384,4]{0,1:T(4,128)S(1)} all-gather(f32[512,4]{0,1:T(4,128)S(1)} %select_reduce_fusion.2), channel_id=2, replica_groups=mesh['pool'=32,'exp'=4] {'pool'}, dimensions={0}, use_global_device_ids=true | all-gather | bytes 270336 | tf_op jit(solution)/shard_map/all_gather | solution.py:26
  110.9 22.9 %all-gather.5.cloned.1.call-done = f32[16384,256]{1,0:T(8,128)} async-done(((f32[512,256]{1,0:T(8,128)}), f32[16384,256]{1,0:T(8,128)}) %all-gather.5.cloned.1.call-update) | async-done | bytes 16777232 | tf_op jit(solution)/shard_map/all_gather | solution.py:26
  133.7 1.1 slice.32
  135.0 11.4 %slice.35 = f32[15872,256]{1,0:T(8,128)} slice(f32[16384,256]{1,0:T(8,128)} %all-gather.5.cloned.1.call-done), slice={[512:16384], [0:256]} | slice | bytes 32505856 | tf_op jit(solution)/shard_map/slice | solution.py:28
  146.4 70.2 %while.14 = (s32[]{:T(128)}, f32[512,4]{0,1:T(4,128)S(1)}, f32[512,4]{0,1:T(4,128)S(1)}, f32[512,256]{0,1:T(8,128)S(1)}, f32[31,512,4]{1,2,0:T(4,128)}, /*index=...) while((s32[]{:T(128)}, f32[512,4]{0,1:T(4,128)S(1)}, f32[512,4]{0,1:T(4,128)S(1)}, ...), condition=%wide.region_8.9_spmd, body=%wide.region_7.8_spmd.sunk | while | flops 405506 | bytes 3752029 | solution.py:29
  146.4 0.8 fusion.82
  147.2 1.1 constant_dynamic-slice_fusion.4
  149.4 1.1 constant_dynamic-slice_fusion.4
  151.7 1.1 constant_dynamic-slice_fusion.4
  153.9 1.1 constant_dynamic-slice_fusion.4
  156.2 1.1 constant_dynamic-slice_fusion.4
  158.5 1.1 constant_dynamic-slice_fusion.4
  160.7 1.1 constant_dynamic-slice_fusion.4
  163.0 1.1 constant_dynamic-slice_fusion.4
  165.3 1.1 constant_dynamic-slice_fusion.4
  167.5 1.1 constant_dynamic-slice_fusion.4
  169.8 1.1 constant_dynamic-slice_fusion.4
  172.1 1.1 constant_dynamic-slice_fusion.4
  174.3 1.1 constant_dynamic-slice_fusion.4
  176.6 1.1 constant_dynamic-slice_fusion.4
  178.8 1.1 constant_dynamic-slice_fusion.4
  181.1 1.1 constant_dynamic-slice_fusion.4
  183.4 1.1 constant_dynamic-slice_fusion.4
  185.6 1.1 constant_dynamic-slice_fusion.4
  187.9 1.1 constant_dynamic-slice_fusion.4
  190.2 1.1 constant_dynamic-slice_fusion.4
  192.4 1.1 constant_dynamic-slice_fusion.4
  194.7 1.1 constant_dynamic-slice_fusion.4
  197.0 1.1 constant_dynamic-slice_fusion.4
  199.2 1.1 constant_dynamic-slice_fusion.4
  201.5 1.1 constant_dynamic-slice_fusion.4
  203.7 1.1 constant_dynamic-slice_fusion.4
  206.0 1.1 constant_dynamic-slice_fusion.4
  208.3 1.1 constant_dynamic-slice_fusion.4
  210.5 1.1 constant_dynamic-slice_fusion.4
  212.8 1.1 constant_dynamic-slice_fusion.4
  215.1 1.1 constant_dynamic-slice_fusion.4
  216.8 0.8 fusion.68
  217.8 37.8 %all-reduce.2.cloned.1.call-done = f32[16,1024]{1,0:T(8,128)} async-done(((f32[16,1024]{1,0:T(8,128)}), f32[16,1024]{1,0:T(8,128)}) %all-reduce.2.cloned.1.call-update) | async-done | bytes 65552 | tf_op jit(solution)/shard_map/psum | solution.py:151
  255.6 1.0 multiply_reduce_fusion
  256.6 1.1 fusion.11
  257.7 9.7 %all-to-all-start.1 = ((bf16[32,8,1024]{2,1,0:T(8,128)(2,1)}), bf16[32,8,1024]{2,1,0:T(8,128)(2,1)S(1)}, u32[]{:S(2)}, u32[]{:S(2)}) async-start(bf16[32,8,1024]{2,1,0:T(8,128)(2,1)} %fusion.11), calls=%async_computation.1 | async-start | bytes 1048576 | tf_op jit(solution)/shard_map/all_to_all | solution.py:170
  267.5 11.5 %all-to-all-done.1 = bf16[32,8,1024]{2,1,0:T(8,128)(2,1)S(1)} async-done(((bf16[32,8,1024]{2,1,0:T(8,128)(2,1)}), bf16[32,8,1024]{2,1,0:T(8,128)(2,1)S(1)}, u32[]{:S(2)}, u32[]{:S(2)}) %all-to-all-start.1) | async-done | bytes 524320 | tf_op jit(solution)/shard_map/all_to_all | solution.py:170
  279.0 1.7 fusion.20
  280.7 2.0 fusion.12
  283.4 3.6 %all-to-all-start.2 = ((bf16[32,8,256]{2,1,0:T(8,128)(2,1)}), bf16[32,8,256]{2,1,0:T(8,128)(2,1)S(1)}, u32[]{:S(2)}, u32[]{:S(2)}) async-start(bf16[32,8,256]{2,1,0:T(8,128)(2,1)} %constant_dynamic-slice_fusion.2), calls=%async_computation.2 | async-start | bytes 262144 | tf_op jit(solution)/shard_map/all_to_all | solution.py:180
  287.3 7.4 %all-to-all-done.2 = bf16[32,8,256]{2,1,0:T(8,128)(2,1)S(1)} async-done(((bf16[32,8,256]{2,1,0:T(8,128)(2,1)}), bf16[32,8,256]{2,1,0:T(8,128)(2,1)S(1)}, u32[]{:S(2)}, u32[]{:S(2)}) %all-to-all-start.2) | async-done | bytes 131104 | tf_op jit(solution)/shard_map/all_to_all | solution.py:180
  294.7 0.8 fusion.17
  (159 shorter events, 42.2 us)
Async XLA Ops:
  6.5 274.1 %copy-start = (bf16[1,512,1024]{2,1,0:T(8,128)(2,1)S(1)}, bf16[1,512,1024]{2,1,0:T(8,128)(2,1)}, u32[]{:S(2)}) copy-start(bf16[1,512,1024]{2,1,0:T(8,128)(2,1)} %param.35) | copy-start | bytes 3145732
  6.5 23.4 %copy-start.8 = (bf16[1024,128]{1,0:T(8,128)(2,1)S(1)}, bf16[1024,128]{1,0:T(8,128)(2,1)}, u32[]{:S(2)}) copy-start(bf16[1024,128]{1,0:T(8,128)(2,1)} %param.28) | copy-start | bytes 786436
  10.2 36.6 %all-to-all-start = ((bf16[32,16,256]{2,1,0:T(8,128)(2,1)}), bf16[32,16,256]{2,1,0:T(8,128)(2,1)S(1)}, u32[]{:S(2)}, u32[]{:S(2)}) async-start(bf16[32,16,256]{2,1,0:T(8,128)(2,1)} %stack.2), calls=%async_computation | async-start | bytes 524288 | tf_op jit(solution)/shard_map/all_to_all | solution.py:17
  19.7 114.0 %all-gather.5.cloned.1.call-start = ((), (), s32[]{:S(2)}) async-start(), calls=%async_computation.4 | async-start | bytes 17301504 | tf_op jit(solution)/shard_map/all_gather | solution.py:26
  19.7 10.2 %copy-start.7 = (bf16[16,128,1024]{2,1,0:T(8,128)(2,1)S(1)}, bf16[16,128,1024]{2,1,0:T(8,128)(2,1)}, u32[]{:S(2)}) copy-start(bf16[16,128,1024]{2,1,0:T(8,128)(2,1)} %param.24) | copy-start | bytes 12582916
  30.0 1.3 copy-start.6
  52.1 6.7 %copy-start.3 = (s32[16,8]{0,1:T(8,128)S(1)}, s32[16,8]{0,1:T(8,128)}, u32[]{:S(2)}) copy-start(s32[16,8]{0,1:T(8,128)} %param.31) | copy-start | bytes 1540
  52.1 7.4 %copy-start.5 = (bf16[1024]{0:T(1024)(128)(2,1)S(1)}, bf16[1024]{0:T(1024)(128)(2,1)}, u32[]{:S(2)}) copy-start(bf16[1024]{0:T(1024)(128)(2,1)} %param.30) | copy-start | bytes 6148
  58.7 196.9 %all-reduce.2.cloned.1.call-start = ((), (), s32[]{:S(2)}) async-start(), calls=%async_computation.3 | async-start | bytes 131072 | tf_op jit(solution)/shard_map/psum | solution.py:151
  146.4 70.4 %copy-start.1 = (bf16[256,1024]{1,0:T(8,128)(2,1)S(1)}, bf16[256,1024]{1,0:T(8,128)(2,1)}, u32[]{:S(2)}) copy-start(bf16[256,1024]{1,0:T(8,128)(2,1)} %param.29) | copy-start | bytes 1572868
  146.4 109.2 %copy-start.2 = (bf16[16,1024]{1,0:T(8,128)(2,1)S(1)}, bf16[16,1024]{1,0:T(8,128)(2,1)}, u32[]{:S(2)}) copy-start(bf16[16,1024]{1,0:T(8,128)(2,1)} %param.19) | copy-start | bytes 98308
  146.4 121.0 %copy-start.4 = (f32[16,8]{0,1:T(8,128)S(1)}, f32[16,8]{0,1:T(8,128)}, u32[]{:S(2)}) copy-start(f32[16,8]{0,1:T(8,128)} %param.32) | copy-start | bytes 1540
  257.7 21.3 %all-to-all-start.1 = ((bf16[32,8,1024]{2,1,0:T(8,128)(2,1)}), bf16[32,8,1024]{2,1,0:T(8,128)(2,1)S(1)}, u32[]{:S(2)}, u32[]{:S(2)}) async-start(bf16[32,8,1024]{2,1,0:T(8,128)(2,1)} %fusion.11), calls=%async_computation.1 | async-start | bytes 1048576 | tf_op jit(solution)/shard_map/all_to_all | solution.py:170
  283.4 11.3 %all-to-all-start.2 = ((bf16[32,8,256]{2,1,0:T(8,128)(2,1)}), bf16[32,8,256]{2,1,0:T(8,128)(2,1)S(1)}, u32[]{:S(2)}, u32[]{:S(2)}) async-start(bf16[32,8,256]{2,1,0:T(8,128)(2,1)} %constant_dynamic-slice_fusion.2), calls=%async_computation.2 | async-start | bytes 262144 | tf_op jit(solution)/shard_map/all_to_all | solution.py:180
Sparse Core Ops, SparseCore 0:
  58.8 74.8 all-gather.4
  217.8 37.7 all-reduce.1
